TPU v7x, 512 devices: a whole 4x8x8 slice. The times are simulated.
512 devices in a mesh: section: 4 (over x), rep: 128 (over y, z, core).
Axes of the slice: x: 4, y: 8, z: 8, core: 2. Of those that a mesh axis runs over, the one named last changes fastest.
Arguments:
- tile_features: bfloat16 [256, 16, 16, 512], P('rep'), may hold values from -6 to 6
- patches: bfloat16 [256, 16, 16, 768], P('rep'), may hold values from -6 to 6
- det_kernel: float32 [4, 7, 7, 512], P('section'), may hold values from -0.875 to 0.875
- det_gain: float32 [4, 512], P('section'), may hold values from 0.1 to 1.9
- det_in: bfloat16 [4, 512, 2048], P('section', None, 'rep'), may hold values from -0.25 to 0.25
- det_out: bfloat16 [4, 2048, 512], P('section', 'rep'), may hold values from -0.125 to 0.125
- det_scale: float32 [4, 512], P('section'), may hold values from 0.3 to 1.5
- cls_embed: bfloat16 [768, 1024], P(None, 'section'), may hold values from -0.21875 to 0.21875
- cls_merge: bfloat16 [512, 1024], P(None, 'section'), may hold values from -0.25 to 0.25
- cls_pos: bfloat16 [196, 1024], P(None, 'section'), may hold values from -3 to 3
- cls_qkv: bfloat16 [1024, 3, 512], P(None, None, 'section'), may hold values from -1.5 to 1.5
- cls_out: bfloat16 [512, 1024], P('section'), may hold values from -0.25 to 0.25
- cls_gain: float32 [2, 1024], replicated, may hold values from 0.1 to 1.9
- crop_plan: int32 [128, 4, 3, 3], P('rep'), may hold values from 0 to 2, as said below
- slot_from: int32 [128, 4], P('rep'), may hold values from 0 to 3, as said below
Outputs:
- crop_class: float32 [128, 4, 1024], P('rep', 'section')
Inputs may be any that keep to these rules, and one draw needn't show every extreme that they name: `crop_plan`: each entry is a micro-batch below 2 followed by a top and a left patch offset of 0 to 2; records that no slot names are arbitrary. `slot_from`: 0 marks an empty slot, 1 a crop from the replica one index lower, 2 the replica's own, 3 one from the replica one index higher; the first replica never has 1 and the last never has 3.
All inputs are finite; a program needn't handle non-finite values.
Results may differ from a plain program's by a relative error of at most 0.004.
Values may be sent and summed in bfloat16 or wider, within the bound.
No kernel may reach another device: no remote copies, remote signals or barrier semaphores. Data moves between devices by JAX's collectives and lax.ppermute only.
A program may use at most 64 MiB of HBM per device.

v0:
```python
import math
import jax
import jax.numpy as jnp
from jax import lax
from jax.sharding import PartitionSpec as P

HEAD_DIM = 64
TILE = 16
CROP = 14
epsilon = 1e-06


def passed_along(block, axis, distance):
    devices = range(lax.axis_size(axis))
    route = [(i - distance, i) for i in devices if i - distance in devices]
    return lax.ppermute(block, axis, route)


def spread(value, axis, source):
    kept = jnp.where(lax.axis_index(axis) == source, value, 0).astype(value.dtype)
    return lax.psum(kept, axis)


def padded_2(block, sides, width):
    for axis, dim in sides:
        count = lax.axis_size(axis)
        forward = [(i, i + 1) for i in range(count - 1)]
        backward = [(target, source) for source, target in forward]
        low = lax.ppermute(
            lax.slice_in_dim(block, block.shape[dim] - width, None, axis=dim), axis, forward
        )
        high = lax.ppermute(lax.slice_in_dim(block, 0, width, axis=dim), axis, backward)
        block = jnp.concatenate([low, block, high], axis=dim)
    return block


def layer_norm(values, gain_row):
    row_mean = jnp.mean(values, axis=-1, keepdims=True)
    centred = values - row_mean
    row_var = jnp.mean(centred * centred, axis=-1, keepdims=True)
    return centred * lax.rsqrt(row_var + epsilon) * gain_row


def detector_block(tile_rows, kernel, gain_row, in_weight, out_weight, scale_row):
    widened = tile_rows.astype(jnp.float32)
    padded = jnp.pad(widened, ((3, 3), (3, 3), (0, 0)))
    conv = jnp.zeros_like(widened)
    for row_shift in range(7):
        for col_shift in range(7):
            conv = (
                conv
                + padded[row_shift : row_shift + TILE, col_shift : col_shift + TILE]
                * kernel[row_shift, col_shift]
            )
    normed = layer_norm(conv, gain_row).astype(jnp.bfloat16).reshape(TILE * TILE, -1)
    hidden = jax.nn.gelu(jnp.dot(normed, in_weight, preferred_element_type=jnp.float32)).astype(
        jnp.bfloat16
    )
    update = jnp.dot(hidden, out_weight, preferred_element_type=jnp.float32).reshape(widened.shape)
    return (widened + scale_row * update).astype(jnp.bfloat16)


def per_device(
    tile_features,
    patches,
    det_kernel,
    det_gain,
    det_in,
    det_out,
    det_scale,
    cls_embed,
    cls_merge,
    cls_pos,
    cls_qkv,
    cls_out,
    cls_gain,
    crop_plan,
    slot_from,
):
    sections = lax.axis_size("section")
    section_num = lax.axis_index("section")
    micro_count = tile_features.shape[0]
    in_whole, out_whole = (
        lax.all_gather(det_in, "rep", axis=2, tiled=True),
        lax.all_gather(det_out, "rep", axis=1, tiled=True),
    )
    kernel = det_kernel[0]
    gain_row = det_gain[0]
    scale_row = det_scale[0]
    in_weight = in_whole[0]
    out_weight = out_whole[0]

    def run_block(operand_tile):
        return detector_block(operand_tile, kernel, gain_row, in_weight, out_weight, scale_row)

    def skip_block(operand_tile):
        return jnp.zeros_like(operand_tile)

    def tick(tick_index, loop_state):
        incoming, finals = loop_state
        micro_num = tick_index - section_num
        is_valid = (micro_num >= 0) & (micro_num < micro_count)
        clipped = jnp.clip(micro_num, 0, micro_count - 1)
        fresh_tile = lax.dynamic_index_in_dim(tile_features, clipped, 0, keepdims=False)
        operand = jnp.where(section_num == 0, fresh_tile, incoming)
        result = lax.cond(is_valid, run_block, skip_block, operand)
        stored = lax.dynamic_update_index_in_dim(finals, result, clipped, 0)
        finals = jnp.where(is_valid & (section_num == sections - 1), stored, finals)
        incoming = passed_along(result, "section", 1)
        return (incoming, finals)

    start_state = (
        jnp.zeros(tile_features.shape[1:], jnp.bfloat16),
        jnp.zeros(tile_features.shape, jnp.bfloat16),
    )
    unused_tile, finals = lax.fori_loop(0, micro_count + sections - 1, tick, start_state)
    finals = spread(finals, "section", sections - 1)
    pixel_width = patches.shape[3]
    feat_width = finals.shape[3]
    full_width = cls_gain.shape[1]
    local_width = cls_embed.shape[1]
    local_heads = cls_qkv.shape[2] // HEAD_DIM
    qkv_flat = cls_qkv.reshape(cls_qkv.shape[0], -1)
    gain_first = lax.dynamic_slice_in_dim(cls_gain[0], section_num * local_width, local_width)
    slot_plan = crop_plan[0]
    source = lax.dynamic_index_in_dim(slot_from[0], section_num, 0, keepdims=False)
    zero_index = jnp.int32(0)

    def cut_crop(record):
        pixel_rows = lax.dynamic_slice(
            patches, (record[0], record[1], record[2], zero_index), (1, CROP, CROP, pixel_width)
        ).reshape(CROP * CROP, pixel_width)
        feat_rows = lax.dynamic_slice(
            finals, (record[0], record[1], record[2], zero_index), (1, CROP, CROP, feat_width)
        ).reshape(CROP * CROP, feat_width)
        return (pixel_rows, feat_rows)

    pixel_rows, feat_rows = jax.vmap(cut_crop)(slot_plan.reshape(-1, 3))
    count = pixel_rows.shape[0]
    widened = (
        jnp.einsum("crp,pd->crd", pixel_rows, cls_embed, preferred_element_type=jnp.float32)
        + jnp.einsum("crp,pd->crd", feat_rows, cls_merge, preferred_element_type=jnp.float32)
        + cls_pos.astype(jnp.float32)[None]
    )
    row_sum, row_square = lax.psum(
        (jnp.sum(widened, axis=-1), jnp.sum(widened * widened, axis=-1)), "section"
    )
    row_mean = row_sum / full_width
    row_var = row_square / full_width - row_mean * row_mean
    attn_part = (
        (widened - row_mean[..., None]) * lax.rsqrt(row_var[..., None] + epsilon) * gain_first
    ).astype(jnp.bfloat16)
    attn_in = lax.all_gather(attn_part, "section", axis=2, tiled=True)
    qkv = jnp.einsum("crd,de->cre", attn_in, qkv_flat, preferred_element_type=jnp.float32).astype(
        jnp.bfloat16
    )
    qkv = qkv.reshape(count, CROP * CROP, 3, local_heads, HEAD_DIM)
    query_rows = qkv[:, :, 0]
    key_rows = qkv[:, :, 1]
    value_rows = qkv[:, :, 2]
    scores = jnp.einsum(
        "cqhd,ckhd->chqk", query_rows, key_rows, preferred_element_type=jnp.float32
    ) * (1.0 / math.sqrt(HEAD_DIM))
    top_score = jnp.max(scores, axis=-1, keepdims=True)
    weights = jnp.exp(scores - top_score)
    probs = (weights / jnp.sum(weights, axis=-1, keepdims=True)).astype(jnp.bfloat16)
    context = jnp.einsum(
        "chqk,ckhd->cqhd", probs, value_rows, preferred_element_type=jnp.float32
    ).astype(jnp.bfloat16)
    context_mean = jnp.mean(context.reshape(count, CROP * CROP, -1).astype(jnp.float32), axis=1)
    context_term = jnp.dot(
        context_mean, cls_out.astype(jnp.float32), precision=lax.Precision.HIGHEST
    )
    token_mean = jnp.mean(widened, axis=1)
    placed = lax.dynamic_update_slice_in_dim(
        jnp.zeros((count, full_width), jnp.float32), token_mean, section_num * local_width, 1
    )
    terms = (placed + context_term).reshape(sections, -1)
    pooled = lax.psum_scatter(terms, "section", scatter_dimension=0, tiled=True).reshape(
        -1, full_width
    )
    results = layer_norm(pooled, cls_gain[1])
    outgoing_results = jnp.stack([results[0], results[2]], axis=0)
    extended_results = padded_2(outgoing_results, (("rep", 0),), 1)
    result = jnp.where(
        source == 1, extended_results[0], jnp.where(source == 3, extended_results[3], results[1])
    )
    result = jnp.where(source == 0, jnp.zeros_like(result), result)
    return result[None, None, :]


def solution(mesh):
    return jax.shard_map(
        per_device,
        mesh=mesh,
        in_specs=(
            P("rep", None, None, None),
            P("rep", None, None, None),
            P("section", None, None, None),
            P("section", None),
            P("section", None, "rep"),
            P("section", "rep", None),
            P("section", None),
            P(None, "section"),
            P(None, "section"),
            P(None, "section"),
            P(None, None, "section"),
            P("section", None),
            P(),
            P("rep", None, None, None),
            P("rep", None),
        ),
        out_specs=P("rep", "section", None),
        check_vma=False,
    )
```

profile of v0, /device:TPU:32, one launch (start us, length us, event | category | flops | bytes accessed | tf_op | source)
XLA Modules:
  0.0 480.8 jit_solution(15910834706224890067)
XLA Ops:
  9.9 52.1 %while.18 = (s32[]{:T(128)}, bf16[2,16,16,768]{3,2,1,0:T(8,128)(2,1)}, s32[12,4]{0,1:T(4,128)S(1)}, bf16[12,1,14,14,768]{4,3,2,1,0:T(8,128)(2,1)}, s32[]{:T(128)}) while((s32[]{:T(128)}, bf16[2,16,16,768]{3,2,1,0:T(8,128)(2,1)}, s32[12,4]{0,1:T(4,128)S(1)}, bf16[12,1,14,14,768]{4,3,2,1,0:T(8,128)(2,1)}, s32[]{:T(128)}) %tuple.126), condition=%wide.while_cond, body=%wide.while_body.sunk | while | flops 2 | bytes 690297 | solution.py:130
  10.6 3.7 bitcast_dynamic-update-slice_fusion.2
  14.9 3.7 bitcast_dynamic-update-slice_fusion.2
  19.2 3.7 bitcast_dynamic-update-slice_fusion.2
  23.6 3.7 bitcast_dynamic-update-slice_fusion.2
  27.9 3.7 bitcast_dynamic-update-slice_fusion.2
  32.3 3.7 bitcast_dynamic-update-slice_fusion.2
  36.6 3.7 bitcast_dynamic-update-slice_fusion.2
  41.0 3.7 bitcast_dynamic-update-slice_fusion.2
  45.3 3.7 bitcast_dynamic-update-slice_fusion.2
  49.6 3.7 bitcast_dynamic-update-slice_fusion.2
  54.0 3.7 bitcast_dynamic-update-slice_fusion.2
  58.3 3.7 bitcast_dynamic-update-slice_fusion.2
  62.0 34.7 %all-gather.4.cloned.1.call-done = bf16[1,512,2048]{1,2,0:T(8,128)(2,1)} async-done(((bf16[1,512,16]{1,2,0:T(8,128)(2,1)}), bf16[1,512,2048]{1,2,0:T(8,128)(2,1)}) %all-gather.4.cloned.1.call-update) | async-done | bytes 2097168 | tf_op jit(solution)/shard_map/all_gather | solution.py:84
  96.7 4.0 copy.39
  100.7 79.0 %all-gather.6.cloned.1.call-done = bf16[1,2048,512]{2,1,0:T(8,128)(2,1)} async-done(((bf16[1,16,512]{2,1,0:T(8,128)(2,1)}), bf16[1,2048,512]{2,1,0:T(8,128)(2,1)}) %all-gather.6.cloned.1.call-update) | async-done | bytes 2097168 | tf_op jit(solution)/shard_map/all_gather | solution.py:85
  179.7 84.6 %while.17 = (s32[]{:T(128)}, bf16[16,16,512]{2,1,0:T(8,128)(2,1)S(1)}, bf16[2,16,16,512]{3,2,1,0:T(8,128)(2,1)S(1)}, s32[]{:T(128)}, pred[]{:T(512)}, /*index=5*...) while((s32[]{:T(128)}, ...), condition=%wide.region_5.6_spmd, body=%wide.region_0.5_spmd.sunk | while | flops 1093009664 | bytes 12373336 | solution.py:116
  179.8 10.3 %conditional.2 = (bf16[16,16,512]{2,1,0:T(8,128)(2,1)}, bf16[1,16,16,512]{3,2,1,0:T(8,128)(2,1)S(1)}) conditional(s32[]{:T(128)} %convert_element_type.74, () %tuple.120, (pred[]{:T(512)}, bf16[2,16,16,512]{3,2,1,0:T(8,128)(2,1)S(1)}, s32[]{:T(128)}, bf16[16,16,512]{2,1,0:T(8,128)(2,1)S(1)}, f32[1,512]{1,0:T(1,128)S(1)}, ...), branch_computations={%region_1.1_spmd, %region_2.4_spmd} | conditional | flops 1092878592 | bytes 10538005 | solution.py:106
  180.0 4.2 fusion.129
  184.6 3.8 fusion.8
  191.5 6.5 %collective-permute-done = bf16[16,16,512]{2,1,0:T(8,128)(2,1)S(1)} collective-permute-done((bf16[16,16,512]{2,1,0:T(8,128)(2,1)}, bf16[16,16,512]{2,1,0:T(8,128)(2,1)S(1)}, u32[]{:S(2)}, u32[]{:S(2)}) %collective-permute-start) | collective-permute-done | bytes 262176 | tf_op jit(solution)/shard_map/while/body/eval_jaxpr/ppermute | solution.py:16
  198.0 10.3 %conditional.2 = (bf16[16,16,512]{2,1,0:T(8,128)(2,1)}, bf16[1,16,16,512]{3,2,1,0:T(8,128)(2,1)S(1)}) conditional(s32[]{:T(128)} %convert_element_type.74, () %tuple.120, (pred[]{:T(512)}, bf16[2,16,16,512]{3,2,1,0:T(8,128)(2,1)S(1)}, s32[]{:T(128)}, bf16[16,16,512]{2,1,0:T(8,128)(2,1)S(1)}, f32[1,512]{1,0:T(1,128)S(1)}, ...), branch_computations={%region_1.1_spmd, %region_2.4_spmd} | conditional | flops 1092878592 | bytes 10538005 | solution.py:106
  198.1 4.2 fusion.129
  202.8 3.8 fusion.8
  208.3 4.3 collective-permute-start
  212.7 5.7 %collective-permute-done = bf16[16,16,512]{2,1,0:T(8,128)(2,1)S(1)} collective-permute-done((bf16[16,16,512]{2,1,0:T(8,128)(2,1)}, bf16[16,16,512]{2,1,0:T(8,128)(2,1)S(1)}, u32[]{:S(2)}, u32[]{:S(2)}) %collective-permute-start) | collective-permute-done | bytes 262176 | tf_op jit(solution)/shard_map/while/body/eval_jaxpr/ppermute | solution.py:16
  219.2 13.9 %collective-permute-start = (bf16[16,16,512]{2,1,0:T(8,128)(2,1)}, bf16[16,16,512]{2,1,0:T(8,128)(2,1)S(1)}, u32[]{:S(2)}, u32[]{:S(2)}) collective-permute-start(bf16[16,16,512]{2,1,0:T(8,128)(2,1)} %get-tuple-element.531), channel_id=1, source_target_pairs={{0,128},{128,256},{256,384},{1,129},{129,257},{257,385},{2,130},{1... | collective-permute-start | bytes 786440 | tf_op jit(solution)/shard_map/while/body/eval_jaxpr/ppermute | solution.py:16
  233.1 4.8 %collective-permute-done = bf16[16,16,512]{2,1,0:T(8,128)(2,1)S(1)} collective-permute-done((bf16[16,16,512]{2,1,0:T(8,128)(2,1)}, bf16[16,16,512]{2,1,0:T(8,128)(2,1)S(1)}, u32[]{:S(2)}, u32[]{:S(2)}) %collective-permute-start) | collective-permute-done | bytes 262176 | tf_op jit(solution)/shard_map/while/body/eval_jaxpr/ppermute | solution.py:16
  238.7 4.3 collective-permute-start
  243.1 4.1 collective-permute-done
  247.9 12.2 %collective-permute-start = (bf16[16,16,512]{2,1,0:T(8,128)(2,1)}, bf16[16,16,512]{2,1,0:T(8,128)(2,1)S(1)}, u32[]{:S(2)}, u32[]{:S(2)}) collective-permute-start(bf16[16,16,512]{2,1,0:T(8,128)(2,1)} %get-tuple-element.531), channel_id=1, source_target_pairs={{0,128},{128,256},{256,384},{1,129},{129,257},{257,385},{2,130},{1... | collective-permute-start | bytes 786440 | tf_op jit(solution)/shard_map/while/body/eval_jaxpr/ppermute | solution.py:16
  260.2 4.1 collective-permute-done
  264.3 1.5 broadcast_select_fusion
  266.1 6.0 %reshape.115 = bf16[12,196,768]{2,1,0:T(8,128)(2,1)} reshape(bf16[12,1,14,14,768]{4,3,2,1,0:T(8,128)(2,1)} %get-tuple-element.289) | data formatting | bytes 7225344 | tf_op jit(solution)/shard_map/vmap()/reshape | solution.py:132
  272.2 3.2 fusion.123
  275.3 52.9 %all-reduce.5.cloned.1.call-done = bf16[2,16,16,512]{3,0,2,1:T(2,128)(2,1)} async-done(((bf16[2,16,16,512]{3,0,2,1:T(2,128)(2,1)}), bf16[2,16,16,512]{3,0,2,1:T(2,128)(2,1)}) %all-reduce.5.cloned.1.call-update) | async-done | bytes 524304 | tf_op jit(solution)/shard_map/psum | solution.py:21
  328.2 12.1 %gather_fusion = bf16[12,14,14,512]{3,0,2,1:T(8,128)(2,1)} fusion(bf16[2,16,16,512]{3,0,2,1:T(2,128)(2,1)} %all-reduce.5.cloned.1.call-done, s32[12]{0:T(128)S(1)} %get-tuple-element.423), kind=kCustom, calls=%fused_computation | custom fusion | bytes 4817088 | tf_op jit(solution)/shard_map/vmap()/gather | solution.py:133
  340.3 6.5 %fusion.128 = (f32[12,256]{1,0:T(8,128)S(1)}, f32[12,196]{1,0:T(8,128)S(1)}, f32[12,196]{1,0:T(8,128)S(1)}, f32[12,196,256]{2,1,0:T(8,128)}) fusion(f32[196,256]{1,0:T(8,128)S(1)} %convert_element_type.50, f32[12,196,256]{2,1,0:T(8,128)S(1)} %fusion.123, bf16[512,256]{1,0:T(8,128)(2,1)S(1)} %copy-done.9, bf16[12,196,512]{2,0,1:T(8,128)(2,1)} %bitcast.131), kind=kOutput, calls=%fused_computation.214 | convolution fusion | flops 620167552 | bytes 7719296 | tf_op jit(solution)/shard_map/crp,pd->crd/dot_general | solution.py:142
  346.7 16.1 %all-reduce.2 = (f32[12,196]{1,0:T(8,128)S(1)}, f32[12,196]{1,0:T(8,128)S(1)}) all-reduce(f32[12,196]{1,0:T(8,128)S(1)} %get-tuple-element.327, f32[12,196]{1,0:T(8,128)S(1)} %get-tuple-element.328), channel_id=1, replica_groups=mesh['section'=4,'rep'=128] {'section'}, use_global_device_ids=true, to_apply=%region_10.11 | all-reduce | flops 4704 | bytes 37632 | tf_op jit(solution)/shard_map/psum | solution.py:145
  362.8 3.0 multiply_convert_fusion.1
  366.2 1.3 dynamic-slice.12
  367.5 61.6 %all-gather.8.cloned.1.call-done = bf16[12,196,1024]{2,1,0:T(8,128)(2,1)} async-done(((bf16[12,196,256]{2,1,0:T(8,128)(2,1)}), bf16[12,196,1024]{2,1,0:T(8,128)(2,1)}) %all-gather.8.cloned.1.call-update) | async-done | bytes 4816912 | tf_op jit(solution)/shard_map/all_gather | solution.py:153
  429.1 6.4 %convolution_convert_fusion = bf16[12,196,384]{2,1,0:T(8,128)(2,1)} fusion(bf16[12,196,1024]{2,1,0:T(8,128)(2,1)} %all-gather.8.cloned.1.call-done, bf16[1024,384,1]{0,1,2:T(8,128)(2,1)S(1)} %bitcast.133), kind=kOutput, calls=%fused_computation.181 | convolution fusion | flops 1850591232 | bytes 7409664 | tf_op jit(solution)/shard_map/crd,de->cre/dot_general | solution.py:154
  435.6 2.7 copy.44
  439.1 4.1 fusion.137
  444.5 16.7 %all-reduce.1 = f32[4,3072]{1,0:T(4,128)S(1)} all-reduce(f32[4,3072]{1,0:T(4,128)S(1)} %reshape.119), channel_id=2, replica_groups=mesh['section'=4,'rep'=128] {'section'}, use_global_device_ids=true, to_apply=%region_15.16.clone | all-reduce | flops 12288 | bytes 98304
  462.3 1.9 collective-permute-start.1
  464.3 7.0 %collective-permute-start.2 = (f32[1,1024]{1,0:T(1,128)S(1)}, f32[1,1024]{1,0:T(1,128)S(1)}, u32[]{:S(2)}, u32[]{:S(2)}) collective-permute-start(f32[1,1024]{1,0:T(1,128)S(1)} %get-tuple-element.417), channel_id=1, source_target_pairs={{1,0},{2,1},{3,2},{4,3},{5,4},{6,5},{7,6},{8,7},{9,8},{10,9},{11,1... | collective-permute-start | bytes 12296 | tf_op jit(solution)/shard_map/ppermute | solution.py:32
  (120 shorter events, 27.7 us)
Async XLA Ops:
  6.5 265.6 %copy-start = (bf16[768,256]{1,0:T(8,128)(2,1)S(1)}, bf16[768,256]{1,0:T(8,128)(2,1)}, u32[]{:S(2)}) copy-start(bf16[768,256]{1,0:T(8,128)(2,1)} %param.26) | copy-start | bytes 1179652
  6.5 90.1 %all-gather.4.cloned.1.call-start = ((), (), s32[]{:S(2)}) async-start(), calls=%async_computation | async-start | bytes 2113536 | tf_op jit(solution)/shard_map/all_gather | solution.py:84
  7.3 172.4 %all-gather.6.cloned.1.call-start = ((), (), s32[]{:S(2)}) async-start(), calls=%async_computation.1 | async-start | bytes 2113536 | tf_op jit(solution)/shard_map/all_gather | solution.py:85
  8.0 320.2 %all-reduce.5.cloned.1.call-start = ((), (), s32[]{:S(2)}) async-start(), calls=%async_computation.2 | async-start | bytes 1048576 | tf_op jit(solution)/shard_map/psum | solution.py:21
  96.7 83.1 %copy-start.1 = (bf16[2,16,16,512]{3,2,1,0:T(8,128)(2,1)S(1)}, bf16[2,16,16,512]{3,2,1,0:T(8,128)(2,1)}, u32[]{:S(2)}) copy-start(bf16[2,16,16,512]{3,2,1,0:T(8,128)(2,1)} %param.19) | copy-start | bytes 1572868
  96.7 83.1 %copy-start.5 = (f32[1,512]{1,0:T(1,128)S(1)}, f32[1,512]{1,0:T(1,128)}, u32[]{:S(2)}) copy-start(f32[1,512]{1,0:T(1,128)} %param.25) | copy-start | bytes 6148
  96.7 83.1 %copy-start.6 = (f32[1,512]{1,0:T(1,128)S(1)}, f32[1,512]{1,0:T(1,128)}, u32[]{:S(2)}) copy-start(f32[1,512]{1,0:T(1,128)} %param.22) | copy-start | bytes 6148
  179.7 86.3 %copy-start.7 = (f32[2,1024]{1,0:T(2,128)S(1)}, f32[2,1024]{1,0:T(2,128)}, u32[]{:S(2)}) copy-start(f32[2,1024]{1,0:T(2,128)} %param.31) | copy-start | bytes 24580
  190.1 7.9 %collective-permute-start = (bf16[16,16,512]{2,1,0:T(8,128)(2,1)}, bf16[16,16,512]{2,1,0:T(8,128)(2,1)S(1)}, u32[]{:S(2)}, u32[]{:S(2)}) collective-permute-start(bf16[16,16,512]{2,1,0:T(8,128)(2,1)} %get-tuple-element.531), channel_id=1, source_target_pairs={{0,128},{128,256},{256,384},{1,129},{129,257},{257,385},{2,130},{1... | collective-permute-start | bytes 786440 | tf_op jit(solution)/shard_map/while/body/eval_jaxpr/ppermute | solution.py:16
  208.3 10.1 %collective-permute-start = (bf16[16,16,512]{2,1,0:T(8,128)(2,1)}, bf16[16,16,512]{2,1,0:T(8,128)(2,1)S(1)}, u32[]{:S(2)}, u32[]{:S(2)}) collective-permute-start(bf16[16,16,512]{2,1,0:T(8,128)(2,1)} %get-tuple-element.531), channel_id=1, source_target_pairs={{0,128},{128,256},{256,384},{1,129},{129,257},{257,385},{2,130},{1... | collective-permute-start | bytes 786440 | tf_op jit(solution)/shard_map/while/body/eval_jaxpr/ppermute | solution.py:16
  219.2 18.8 %collective-permute-start = (bf16[16,16,512]{2,1,0:T(8,128)(2,1)}, bf16[16,16,512]{2,1,0:T(8,128)(2,1)S(1)}, u32[]{:S(2)}, u32[]{:S(2)}) collective-permute-start(bf16[16,16,512]{2,1,0:T(8,128)(2,1)} %get-tuple-element.531), channel_id=1, source_target_pairs={{0,128},{128,256},{256,384},{1,129},{129,257},{257,385},{2,130},{1... | collective-permute-start | bytes 786440 | tf_op jit(solution)/shard_map/while/body/eval_jaxpr/ppermute | solution.py:16
  238.7 8.5 %collective-permute-start = (bf16[16,16,512]{2,1,0:T(8,128)(2,1)}, bf16[16,16,512]{2,1,0:T(8,128)(2,1)S(1)}, u32[]{:S(2)}, u32[]{:S(2)}) collective-permute-start(bf16[16,16,512]{2,1,0:T(8,128)(2,1)} %get-tuple-element.531), channel_id=1, source_target_pairs={{0,128},{128,256},{256,384},{1,129},{129,257},{257,385},{2,130},{1... | collective-permute-start | bytes 786440 | tf_op jit(solution)/shard_map/while/body/eval_jaxpr/ppermute | solution.py:16
  247.9 16.4 %collective-permute-start = (bf16[16,16,512]{2,1,0:T(8,128)(2,1)}, bf16[16,16,512]{2,1,0:T(8,128)(2,1)S(1)}, u32[]{:S(2)}, u32[]{:S(2)}) collective-permute-start(bf16[16,16,512]{2,1,0:T(8,128)(2,1)} %get-tuple-element.531), channel_id=1, source_target_pairs={{0,128},{128,256},{256,384},{1,129},{129,257},{257,385},{2,130},{1... | collective-permute-start | bytes 786440 | tf_op jit(solution)/shard_map/while/body/eval_jaxpr/ppermute | solution.py:16
  265.8 163.3 %all-gather.8.cloned.1.call-start = ((), (), s32[]{:S(2)}) async-start(), calls=%async_computation.3 | async-start | bytes 6144000 | tf_op jit(solution)/shard_map/all_gather | solution.py:153
  266.1 6.0 %copy-start.4 = (bf16[196,256]{1,0:T(8,128)(2,1)S(1)}, bf16[196,256]{1,0:T(8,128)(2,1)}, u32[]{:S(2)}) copy-start(bf16[196,256]{1,0:T(8,128)(2,1)} %param.28) | copy-start | bytes 301060
  328.2 12.1 %copy-start.9 = (bf16[512,256]{1,0:T(8,128)(2,1)S(1)}, bf16[512,256]{1,0:T(8,128)(2,1)}, u32[]{:S(2)}) copy-start(bf16[512,256]{1,0:T(8,128)(2,1)} %param.27) | copy-start | bytes 786436
  362.8 3.1 copy-start.2
  443.3 1.0 copy-start.3
  443.3 28.0 %copy-start.8 = (s32[1,4]{1,0:T(1,128)S(1)}, s32[1,4]{1,0:T(1,128)}, u32[]{:S(2)}) copy-start(s32[1,4]{1,0:T(1,128)} %param.33) | copy-start | bytes 52
  462.3 10.8 %collective-permute-start.1 = (f32[1,1024]{1,0:T(1,128)S(1)}, f32[1,1024]{1,0:T(1,128)S(1)}, u32[]{:S(2)}, u32[]{:S(2)}) collective-permute-start(f32[1,1024]{1,0:T(1,128)S(1)} %get-tuple-element.418), channel_id=1, source_target_pairs={{0,1},{1,2},{2,3},{3,4},{4,5},{5,6},{6,7},{7,8},{8,9},{9,10},{10,1... | collective-permute-start | bytes 12296 | tf_op jit(solution)/shard_map/ppermute | solution.py:29
  464.3 8.9 %collective-permute-start.2 = (f32[1,1024]{1,0:T(1,128)S(1)}, f32[1,1024]{1,0:T(1,128)S(1)}, u32[]{:S(2)}, u32[]{:S(2)}) collective-permute-start(f32[1,1024]{1,0:T(1,128)S(1)} %get-tuple-element.417), channel_id=1, source_target_pairs={{1,0},{2,1},{3,2},{4,3},{5,4},{6,5},{7,6},{8,7},{9,8},{10,9},{11,1... | collective-permute-start | bytes 12296 | tf_op jit(solution)/shard_map/ppermute | solution.py:32
Sparse Core Ops, SparseCore 0:
  10.5 86.1 all-gather.3
  99.8 79.7 all-gather.5
  265.9 62.2 all-reduce.4
  366.0 63.1 all-gather.7
where the time goes:
time: 482 us; the launch traced here: 481 us
  waiting for transfers between devices  255 us (53%)
  local copies, waits for them, and re-layouts  85.6 us (18%)
  starting transfers between devices  45.1 us (9%)
  blocking collectives  32.7 us (7%)
  matrix products  25.5 us (5%)
  other arithmetic  22.2 us (5%)
  between operations  14.8 us (3%)
    all_gather x1, waiting for transfers between devices, per_device(): lax.all_gather(det_out, 'rep', axis=1, tiled=True)  79 us
    all_gather x1, waiting for transfers between devices, per_device(): attn_in = lax.all_gather(attn_part, 'section', axis=2, tiled=True)  61.6 us
    psum x1, waiting for transfers between devices, spread(): return lax.psum(kept, axis)  52.9 us
    gather x36, local copies, waits for them, and re-layouts  52 us
    ppermute x5, starting transfers between devices, passed_along(): return lax.ppermute(block, axis, route)  35.9 us
    all_gather x1, waiting for transfers between devices, per_device(): lax.all_gather(det_in, 'rep', axis=2, tiled=True)  34.7 us
    ppermute x5, waiting for transfers between devices, passed_along(): return lax.ppermute(block, axis, route)  25.1 us
    unnamed x1, blocking collectives  16.7 us
  transfers between devices with their start and end apart: 11, of which 9 were waited for; matrix products, arithmetic and copies ran while one was open for 15% of the time, Pallas kernels for 0%

commit v1 on v0

--- a/solution.py
+++ b/solution.py
@@ -81,7 +81,9 @@
     section_num = lax.axis_index("section")
     micro_count = tile_features.shape[0]
     in_whole, out_whole = (
-        lax.all_gather(det_in, "rep", axis=2, tiled=True),
+        jnp.concatenate(
+            lax.all_to_all(jnp.stack([det_in] * lax.axis_size("rep")), "rep", 0, 0), axis=2
+        ),
         lax.all_gather(det_out, "rep", axis=1, tiled=True),
     )
     kernel = det_kernel[0]

time: 482 us -> 457 us (0.948)
  waiting for transfers between devices: 255 us -> 190 us
  starting transfers between devices: 45.1 us -> 70.9 us
  local copies, waits for them, and re-layouts: 85.6 us -> 92.8 us
    all_gather x1 -> x0, waiting for transfers between devices: 34.7 us -> none  [per_device(): lax.all_gather(det_in, 'rep', axis=2, tiled=True)]
    all_gather x1, waiting for transfers between devices: 79 us -> 48.2 us  [per_device(): lax.all_gather(det_out, 'rep', axis=1, tiled=True)]
    all_to_all x0 -> x1, starting transfers between devices: none -> 17.5 us  [per_device(): lax.all_to_all(jnp.stack([det_in] * lax.axis_size('rep')), 'rep', 0, 0)]
    ppermute x5, starting transfers between devices: 35.9 us -> 44.2 us  [passed_along(): return lax.ppermute(block, axis, route)]
    slice x6, local copies, waits for them, and re-layouts: 0.17 us -> 6.53 us  [detector_block(): kernel[row_shift, col_shift]]
  transfers between devices with their start and end apart: 11 -> 11, of which waited for: 9 -> 8; matrix products, arithmetic and copies ran while one was open for 15% -> 16% of each run, Pallas kernels for 0% -> 0%
where the time goes in v1:
time: 457 us; the launch traced here: 455 us
  waiting for transfers between devices  190 us (42%)
  local copies, waits for them, and re-layouts  92.8 us (20%)
  starting transfers between devices  70.9 us (16%)
  blocking collectives  32.7 us (7%)
  matrix products  29.1 us (6%)
  other arithmetic  24.1 us (5%)
  between operations  14.7 us (3%)
    all_gather x1, waiting for transfers between devices, per_device(): attn_in = lax.all_gather(attn_part, 'section', axis=2, tiled=True)  60.9 us
    psum x1, waiting for transfers between devices, spread(): return lax.psum(kept, axis)  55.4 us
    gather x36, local copies, waits for them, and re-layouts  53.4 us
    all_gather x1, waiting for transfers between devices, per_device(): lax.all_gather(det_out, 'rep', axis=1, tiled=True)  48.2 us
    ppermute x5, starting transfers between devices, passed_along(): return lax.ppermute(block, axis, route)  44.2 us
    ppermute x5, waiting for transfers between devices, passed_along(): return lax.ppermute(block, axis, route)  25.1 us
    all_to_all x1, starting transfers between devices, per_device(): lax.all_to_all(jnp.stack([det_in] * lax.axis_size('rep')), 'rep', 0, 0)  17.5 us
    unnamed x1, blocking collectives  16.7 us
  transfers between devices with their start and end apart: 11, of which 8 were waited for; matrix products, arithmetic and copies ran while one was open for 16% of the time, Pallas kernels for 0%

profile of v1, /device:TPU:32, one launch (start us, length us, event | category | flops | bytes accessed | tf_op | source)
XLA Modules:
  0.0 455.0 jit_solution(10776315489887064994)
XLA Ops:
  6.5 2.4 stack.2
  8.9 17.5 %all-to-all-start = ((bf16[128,1,512,16]{2,3,1,0:T(8,128)(2,1)}), bf16[128,1,512,16]{2,3,1,0:T(8,128)(2,1)S(1)}, u32[]{:S(2)}, u32[]{:S(2)}) async-start(bf16[128,1,512,16]{2,3,1,0:T(8,128)(2,1)} %stack.2), calls=%async_computation | async-start | bytes 4194304 | tf_op jit(solution)/shard_map/all_to_all | solution.py:85
  28.1 53.4 %while.18 = (s32[]{:T(128)}, bf16[2,16,16,768]{3,2,1,0:T(8,128)(2,1)}, s32[12,4]{0,1:T(4,128)S(1)}, bf16[12,1,14,14,768]{4,3,2,1,0:T(8,128)(2,1)}, s32[]{:T(128)}) while((s32[]{:T(128)}, bf16[2,16,16,768]{3,2,1,0:T(8,128)(2,1)}, s32[12,4]{0,1:T(4,128)S(1)}, bf16[12,1,14,14,768]{4,3,2,1,0:T(8,128)(2,1)}, s32[]{:T(128)}) %tuple.126), condition=%wide.while_cond, body=%wide.while_body.sunk | while | flops 2 | bytes 690297 | solution.py:132
  28.8 3.8 bitcast_dynamic-update-slice_fusion.2
  33.2 3.8 bitcast_dynamic-update-slice_fusion.2
  37.7 3.8 bitcast_dynamic-update-slice_fusion.2
  42.1 3.8 bitcast_dynamic-update-slice_fusion.2
  46.6 3.8 bitcast_dynamic-update-slice_fusion.2
  51.0 3.8 bitcast_dynamic-update-slice_fusion.2
  55.5 3.8 bitcast_dynamic-update-slice_fusion.2
  60.0 3.8 bitcast_dynamic-update-slice_fusion.2
  64.4 3.8 bitcast_dynamic-update-slice_fusion.2
  68.8 3.8 bitcast_dynamic-update-slice_fusion.2
  73.3 3.8 bitcast_dynamic-update-slice_fusion.2
  77.7 3.8 bitcast_dynamic-update-slice_fusion.2
  81.5 2.5 copy.40
  84.0 48.2 %all-gather.3.cloned.1.call-done = bf16[1,2048,512]{2,1,0:T(8,128)(2,1)} async-done(((bf16[1,16,512]{2,1,0:T(8,128)(2,1)}), bf16[1,2048,512]{2,1,0:T(8,128)(2,1)}) %all-gather.3.cloned.1.call-update) | async-done | bytes 2097168 | tf_op jit(solution)/shard_map/all_gather | solution.py:87
  132.3 101.3 %while.17 = (s32[]{:T(128)}, bf16[16,16,512]{2,1,0:T(8,128)(2,1)S(1)}, bf16[2,16,16,512]{3,2,1,0:T(8,128)(2,1)S(1)}, s32[]{:T(128)}, pred[]{:T(512)}, /*index=5*...) while((s32[]{:T(128)}, ...), condition=%wide.region_5.6_spmd, body=%wide.region_0.5_spmd.sunk | while | flops 1093009664 | bytes 12373336 | solution.py:118
  132.3 14.5 %conditional.2 = (bf16[16,16,512]{2,1,0:T(8,128)(2,1)}, bf16[1,16,16,512]{3,2,1,0:T(8,128)(2,1)S(1)}) conditional(s32[]{:T(128)} %convert_element_type.74, () %tuple.120, (pred[]{:T(512)}, bf16[2,16,16,512]{3,2,1,0:T(8,128)(2,1)}, s32[]{:T(128)}, bf16[16,16,512]{2,1,0:T(8,128)(2,1)S(1)}, f32[1,512]{1,0:T(1,128)S(1)}, ...), branch_computations={%region_1.1_spmd, %region_2.4_spmd} | conditional | flops 1092878592 | bytes 10538005 | solution.py:108
  136.6 4.2 fusion.129
  141.2 3.8 fusion.8
  148.2 6.5 %collective-permute-done = bf16[16,16,512]{2,1,0:T(8,128)(2,1)S(1)} collective-permute-done((bf16[16,16,512]{2,1,0:T(8,128)(2,1)}, bf16[16,16,512]{2,1,0:T(8,128)(2,1)S(1)}, u32[]{:S(2)}, u32[]{:S(2)}) %collective-permute-start) | collective-permute-done | bytes 262176 | tf_op jit(solution)/shard_map/while/body/eval_jaxpr/ppermute | solution.py:16
  154.7 14.5 %conditional.2 = (bf16[16,16,512]{2,1,0:T(8,128)(2,1)}, bf16[1,16,16,512]{3,2,1,0:T(8,128)(2,1)S(1)}) conditional(s32[]{:T(128)} %convert_element_type.74, () %tuple.120, (pred[]{:T(512)}, bf16[2,16,16,512]{3,2,1,0:T(8,128)(2,1)}, s32[]{:T(128)}, bf16[16,16,512]{2,1,0:T(8,128)(2,1)S(1)}, f32[1,512]{1,0:T(1,128)S(1)}, ...), branch_computations={%region_1.1_spmd, %region_2.4_spmd} | conditional | flops 1092878592 | bytes 10538005 | solution.py:108
  159.0 4.2 fusion.129
  163.6 3.8 fusion.8
  169.2 4.3 collective-permute-start
  173.6 5.7 %collective-permute-done = bf16[16,16,512]{2,1,0:T(8,128)(2,1)S(1)} collective-permute-done((bf16[16,16,512]{2,1,0:T(8,128)(2,1)}, bf16[16,16,512]{2,1,0:T(8,128)(2,1)S(1)}, u32[]{:S(2)}, u32[]{:S(2)}) %collective-permute-start) | collective-permute-done | bytes 262176 | tf_op jit(solution)/shard_map/while/body/eval_jaxpr/ppermute | solution.py:16
  180.0 18.0 %collective-permute-start = (bf16[16,16,512]{2,1,0:T(8,128)(2,1)}, bf16[16,16,512]{2,1,0:T(8,128)(2,1)S(1)}, u32[]{:S(2)}, u32[]{:S(2)}) collective-permute-start(bf16[16,16,512]{2,1,0:T(8,128)(2,1)} %get-tuple-element.531), channel_id=1, source_target_pairs={{0,128},{128,256},{256,384},{1,129},{129,257},{257,385},{2,130},{1... | collective-permute-start | bytes 786440 | tf_op jit(solution)/shard_map/while/body/eval_jaxpr/ppermute | solution.py:16
  198.1 4.8 %collective-permute-done = bf16[16,16,512]{2,1,0:T(8,128)(2,1)S(1)} collective-permute-done((bf16[16,16,512]{2,1,0:T(8,128)(2,1)}, bf16[16,16,512]{2,1,0:T(8,128)(2,1)S(1)}, u32[]{:S(2)}, u32[]{:S(2)}) %collective-permute-start) | collective-permute-done | bytes 262176 | tf_op jit(solution)/shard_map/while/body/eval_jaxpr/ppermute | solution.py:16
  203.7 4.3 collective-permute-start
  208.1 4.1 collective-permute-done
  213.0 16.4 %collective-permute-start = (bf16[16,16,512]{2,1,0:T(8,128)(2,1)}, bf16[16,16,512]{2,1,0:T(8,128)(2,1)S(1)}, u32[]{:S(2)}, u32[]{:S(2)}) collective-permute-start(bf16[16,16,512]{2,1,0:T(8,128)(2,1)} %get-tuple-element.531), channel_id=1, source_target_pairs={{0,128},{128,256},{256,384},{1,129},{129,257},{257,385},{2,130},{1... | collective-permute-start | bytes 786440 | tf_op jit(solution)/shard_map/while/body/eval_jaxpr/ppermute | solution.py:16
  229.5 4.1 collective-permute-done
  235.3 6.1 %reshape.121 = bf16[12,196,768]{2,1,0:T(8,128)(2,1)} reshape(bf16[12,1,14,14,768]{4,3,2,1,0:T(8,128)(2,1)} %get-tuple-element.289) | data formatting | bytes 7225344 | tf_op jit(solution)/shard_map/vmap()/reshape | solution.py:134
  241.4 4.6 %fusion.123 = f32[12,196,256]{2,1,0:T(8,128)} fusion(bf16[12,196,768]{2,1,0:T(8,128)(2,1)} %reshape.121, bf16[768,256]{1,0:T(8,128)(2,1)S(1)} %copy-done), kind=kOutput, calls=%fused_computation.189 | convolution fusion | flops 924844032 | bytes 6414336 | tf_op jit(solution)/shard_map/crp,pd->crd/dot_general | solution.py:143
  246.0 55.4 %all-reduce.5.cloned.1.call-done = bf16[2,16,16,512]{3,0,2,1:T(2,128)(2,1)} async-done(((bf16[2,16,16,512]{3,0,2,1:T(2,128)(2,1)}), bf16[2,16,16,512]{3,0,2,1:T(2,128)(2,1)}) %all-reduce.5.cloned.1.call-update) | async-done | bytes 524304 | tf_op jit(solution)/shard_map/psum | solution.py:21
  301.4 11.1 %gather_fusion = bf16[12,14,14,512]{3,0,2,1:T(8,128)(2,1)} fusion(bf16[2,16,16,512]{3,0,2,1:T(2,128)(2,1)} %all-reduce.5.cloned.1.call-done, s32[12]{0:T(128)S(1)} %get-tuple-element.423), kind=kCustom, calls=%fused_computation | custom fusion | bytes 4817088 | tf_op jit(solution)/shard_map/vmap()/gather | solution.py:135
  312.5 7.2 %fusion.128 = (f32[12,256]{1,0:T(8,128)S(1)}, f32[12,196]{1,0:T(8,128)S(1)}, f32[12,196]{1,0:T(8,128)S(1)}, f32[12,196,256]{2,1,0:T(8,128)}) fusion(f32[196,256]{1,0:T(8,128)S(1)} %convert_element_type.50, f32[12,196,256]{2,1,0:T(8,128)} %fusion.123, bf16[512,256]{1,0:T(8,128)(2,1)S(1)} %copy-done.10, bf16[12,196,512]{2,0,1:T(8,128)(2,1)} %bitcast.137), kind=kOutput, calls=%fused_computation.214 | convolution fusion | flops 620167552 | bytes 7719296 | tf_op jit(solution)/shard_map/crp,pd->crd/dot_general | solution.py:144
  319.7 16.1 %all-reduce.2 = (f32[12,196]{1,0:T(8,128)S(1)}, f32[12,196]{1,0:T(8,128)S(1)}) all-reduce(f32[12,196]{1,0:T(8,128)S(1)} %get-tuple-element.327, f32[12,196]{1,0:T(8,128)S(1)} %get-tuple-element.328), channel_id=1, replica_groups=mesh['section'=4,'rep'=128] {'section'}, use_global_device_ids=true, to_apply=%region_10.11 | all-reduce | flops 4704 | bytes 37632 | tf_op jit(solution)/shard_map/psum | solution.py:147
  335.8 3.0 multiply_convert_fusion.1
  341.3 60.9 %all-gather.5.cloned.1.call-done = bf16[12,196,1024]{2,1,0:T(8,128)(2,1)} async-done(((bf16[12,196,256]{2,1,0:T(8,128)(2,1)}), bf16[12,196,1024]{2,1,0:T(8,128)(2,1)}) %all-gather.5.cloned.1.call-update) | async-done | bytes 4816912 | tf_op jit(solution)/shard_map/all_gather | solution.py:155
  402.2 5.4 %convolution_convert_fusion = bf16[12,196,384]{2,1,0:T(8,128)(2,1)S(1)} fusion(bf16[12,196,1024]{2,1,0:T(8,128)(2,1)} %all-gather.5.cloned.1.call-done, bf16[1024,384,1]{0,1,2:T(8,128)(2,1)} %bitcast.138), kind=kOutput, calls=%fused_computation.181 | convolution fusion | flops 1850591232 | bytes 7409664 | tf_op jit(solution)/shard_map/crd,de->cre/dot_general | solution.py:156
  407.6 2.5 copy.45
  410.1 2.2 fusion.122
  412.3 4.1 fusion.137
  416.4 1.9 convert_reduce_fusion
  418.7 16.7 %all-reduce.1 = f32[4,3072]{1,0:T(4,128)S(1)} all-reduce(f32[4,3072]{1,0:T(4,128)S(1)} %reshape.126), channel_id=2, replica_groups=mesh['section'=4,'rep'=128] {'section'}, use_global_device_ids=true, to_apply=%region_15.16.clone | all-reduce | flops 12288 | bytes 98304
  438.4 7.0 %collective-permute-start.2 = (f32[1,1024]{1,0:T(1,128)S(1)}, f32[1,1024]{1,0:T(1,128)S(1)}, u32[]{:S(2)}, u32[]{:S(2)}) collective-permute-start(f32[1,1024]{1,0:T(1,128)S(1)} %get-tuple-element.417), channel_id=1, source_target_pairs={{1,0},{2,1},{3,2},{4,3},{5,4},{6,5},{7,6},{8,7},{9,8},{10,9},{11,1... | collective-permute-start | bytes 12296 | tf_op jit(solution)/shard_map/ppermute | solution.py:32
  (122 shorter events, 38.2 us)
Async XLA Ops:
  6.5 234.9 %copy-start = (bf16[768,256]{1,0:T(8,128)(2,1)S(1)}, bf16[768,256]{1,0:T(8,128)(2,1)}, u32[]{:S(2)}) copy-start(bf16[768,256]{1,0:T(8,128)(2,1)} %param.26) | copy-start | bytes 1179652
  8.9 18.3 %copy-start.8 = (s32[1,4,3,3]{1,0,3,2:T(1,128)S(1)}, s32[1,4,3,3]{1,0,3,2:T(1,128)}, u32[]{:S(2)}) copy-start(s32[1,4,3,3]{1,0,3,2:T(1,128)} %param.32) | copy-start | bytes 436
  8.9 18.5 %copy-start.4 = (f32[1,7,7,512]{3,0,2,1:T(1,128)S(1)}, f32[1,7,7,512]{3,0,2,1:T(1,128)}, u32[]{:S(2)}) copy-start(f32[1,7,7,512]{3,0,2,1:T(1,128)} %param.21) | copy-start | bytes 301060
  8.9 72.6 %all-to-all-start = ((bf16[128,1,512,16]{2,3,1,0:T(8,128)(2,1)}), bf16[128,1,512,16]{2,3,1,0:T(8,128)(2,1)S(1)}, u32[]{:S(2)}, u32[]{:S(2)}) async-start(bf16[128,1,512,16]{2,3,1,0:T(8,128)(2,1)} %stack.2), calls=%async_computation | async-start | bytes 4194304 | tf_op jit(solution)/shard_map/all_to_all | solution.py:85
  26.4 105.8 %all-gather.3.cloned.1.call-start = ((), (), s32[]{:S(2)}) async-start(), calls=%async_computation.1 | async-start | bytes 2113536 | tf_op jit(solution)/shard_map/all_gather | solution.py:87
  27.1 274.3 %all-reduce.5.cloned.1.call-start = ((), (), s32[]{:S(2)}) async-start(), calls=%async_computation.2 | async-start | bytes 1048576 | tf_op jit(solution)/shard_map/psum | solution.py:21
  81.5 50.7 %copy-start.5 = (f32[1,512]{1,0:T(1,128)S(1)}, f32[1,512]{1,0:T(1,128)}, u32[]{:S(2)}) copy-start(f32[1,512]{1,0:T(1,128)} %param.25) | copy-start | bytes 6148
  81.5 50.8 %copy-start.6 = (f32[1,512]{1,0:T(1,128)S(1)}, f32[1,512]{1,0:T(1,128)}, u32[]{:S(2)}) copy-start(f32[1,512]{1,0:T(1,128)} %param.22) | copy-start | bytes 6148
  132.3 103.0 %copy-start.7 = (f32[2,1024]{1,0:T(2,128)S(1)}, f32[2,1024]{1,0:T(2,128)}, u32[]{:S(2)}) copy-start(f32[2,1024]{1,0:T(2,128)} %param.31) | copy-start | bytes 24580
  146.8 7.9 %collective-permute-start = (bf16[16,16,512]{2,1,0:T(8,128)(2,1)}, bf16[16,16,512]{2,1,0:T(8,128)(2,1)S(1)}, u32[]{:S(2)}, u32[]{:S(2)}) collective-permute-start(bf16[16,16,512]{2,1,0:T(8,128)(2,1)} %get-tuple-element.531), channel_id=1, source_target_pairs={{0,128},{128,256},{256,384},{1,129},{129,257},{257,385},{2,130},{1... | collective-permute-start | bytes 786440 | tf_op jit(solution)/shard_map/while/body/eval_jaxpr/ppermute | solution.py:16
  169.2 10.1 %collective-permute-start = (bf16[16,16,512]{2,1,0:T(8,128)(2,1)}, bf16[16,16,512]{2,1,0:T(8,128)(2,1)S(1)}, u32[]{:S(2)}, u32[]{:S(2)}) collective-permute-start(bf16[16,16,512]{2,1,0:T(8,128)(2,1)} %get-tuple-element.531), channel_id=1, source_target_pairs={{0,128},{128,256},{256,384},{1,129},{129,257},{257,385},{2,130},{1... | collective-permute-start | bytes 786440 | tf_op jit(solution)/shard_map/while/body/eval_jaxpr/ppermute | solution.py:16
  180.0 22.9 %collective-permute-start = (bf16[16,16,512]{2,1,0:T(8,128)(2,1)}, bf16[16,16,512]{2,1,0:T(8,128)(2,1)S(1)}, u32[]{:S(2)}, u32[]{:S(2)}) collective-permute-start(bf16[16,16,512]{2,1,0:T(8,128)(2,1)} %get-tuple-element.531), channel_id=1, source_target_pairs={{0,128},{128,256},{256,384},{1,129},{129,257},{257,385},{2,130},{1... | collective-permute-start | bytes 786440 | tf_op jit(solution)/shard_map/while/body/eval_jaxpr/ppermute | solution.py:16
  203.7 8.5 %collective-permute-start = (bf16[16,16,512]{2,1,0:T(8,128)(2,1)}, bf16[16,16,512]{2,1,0:T(8,128)(2,1)S(1)}, u32[]{:S(2)}, u32[]{:S(2)}) collective-permute-start(bf16[16,16,512]{2,1,0:T(8,128)(2,1)} %get-tuple-element.531), channel_id=1, source_target_pairs={{0,128},{128,256},{256,384},{1,129},{129,257},{257,385},{2,130},{1... | collective-permute-start | bytes 786440 | tf_op jit(solution)/shard_map/while/body/eval_jaxpr/ppermute | solution.py:16
  213.0 20.6 %collective-permute-start = (bf16[16,16,512]{2,1,0:T(8,128)(2,1)}, bf16[16,16,512]{2,1,0:T(8,128)(2,1)S(1)}, u32[]{:S(2)}, u32[]{:S(2)}) collective-permute-start(bf16[16,16,512]{2,1,0:T(8,128)(2,1)} %get-tuple-element.531), channel_id=1, source_target_pairs={{0,128},{128,256},{256,384},{1,129},{129,257},{257,385},{2,130},{1... | collective-permute-start | bytes 786440 | tf_op jit(solution)/shard_map/while/body/eval_jaxpr/ppermute | solution.py:16
  235.0 167.2 %all-gather.5.cloned.1.call-start = ((), (), s32[]{:S(2)}) async-start(), calls=%async_computation.3 | async-start | bytes 6144000 | tf_op jit(solution)/shard_map/all_gather | solution.py:155
  235.3 6.1 %copy-start.3 = (bf16[196,256]{1,0:T(8,128)(2,1)S(1)}, bf16[196,256]{1,0:T(8,128)(2,1)}, u32[]{:S(2)}) copy-start(bf16[196,256]{1,0:T(8,128)(2,1)} %param.28) | copy-start | bytes 301060
  301.4 11.1 %copy-start.10 = (bf16[512,256]{1,0:T(8,128)(2,1)S(1)}, bf16[512,256]{1,0:T(8,128)(2,1)}, u32[]{:S(2)}) copy-start(bf16[512,256]{1,0:T(8,128)(2,1)} %param.27) | copy-start | bytes 786436
  335.8 3.1 copy-start.1
  416.4 2.1 copy-start.2
  416.4 29.0 %copy-start.9 = (s32[1,4]{1,0:T(1,128)S(1)}, s32[1,4]{1,0:T(1,128)}, u32[]{:S(2)}) copy-start(s32[1,4]{1,0:T(1,128)} %param.33) | copy-start | bytes 52
  436.5 10.8 %collective-permute-start.1 = (f32[1,1024]{1,0:T(1,128)S(1)}, f32[1,1024]{1,0:T(1,128)S(1)}, u32[]{:S(2)}, u32[]{:S(2)}) collective-permute-start(f32[1,1024]{1,0:T(1,128)S(1)} %get-tuple-element.418), channel_id=1, source_target_pairs={{0,1},{1,2},{2,3},{3,4},{4,5},{5,6},{6,7},{7,8},{8,9},{9,10},{10,1... | collective-permute-start | bytes 12296 | tf_op jit(solution)/shard_map/ppermute | solution.py:29
  438.4 8.9 %collective-permute-start.2 = (f32[1,1024]{1,0:T(1,128)S(1)}, f32[1,1024]{1,0:T(1,128)S(1)}, u32[]{:S(2)}, u32[]{:S(2)}) collective-permute-start(f32[1,1024]{1,0:T(1,128)S(1)} %get-tuple-element.417), channel_id=1, source_target_pairs={{1,0},{2,1},{3,2},{4,3},{5,4},{6,5},{7,6},{8,7},{9,8},{10,9},{11,1... | collective-permute-start | bytes 12296 | tf_op jit(solution)/shard_map/ppermute | solution.py:32
Sparse Core Ops, SparseCore 0:
  30.4 101.7 all-gather.2
  235.1 66.2 all-reduce.4
  339.0 63.2 all-gather.4
